TPU v7x, 32 devices: a whole 2x2x4 slice. The times are simulated.
32 devices in a mesh: tm: 2 (over x), grid: 16 (over z, y, core).
Axes of the slice: x: 2, y: 2, z: 4, core: 2. Of those that a mesh axis runs over, the one named last changes fastest.
Arguments:
- occupied_green: bfloat16 [2, 1024, 1024], P('tm', 'grid'), may hold values from -0.005859375 to 0.005859375
- empty_green: bfloat16 [2, 1024, 1024], P('tm', 'grid'), may hold values from -0.005859375 to 0.005859375
- basis: bfloat16 [12288, 1024], P('grid'), may hold values from -8 to 8
- time_weights: float32 [2, 2], replicated, may hold values from 0.25 to 1
Outputs:
- polarizability: float32 [2, 1024, 1024], P('tm', 'grid')
All inputs are finite; a program needn't handle non-finite values.
Results may differ from a plain program's by a relative error of at most 0.0012.
Values may be sent and summed in bfloat16 or wider, within the bound.
A program may use at most 128 MiB of HBM per device.

v0:
```python
import jax
import jax.numpy as jnp
from jax import lax
from jax.sharding import PartitionSpec as P

NR = 12288
NB = 1024


def weigh_times(time_weights, block_list, scale_factor):
    time_count = len(block_list)
    group_index = lax.axis_index("tm")
    weights_local = lax.dynamic_slice_in_dim(time_weights, group_index * time_count, time_count, 1)
    accum = weights_local[:, 0, None, None] * block_list[0][None]
    return scale_factor * accum


def step_size(piece_rows):
    return max((divisor for divisor in range(1, 2049) if piece_rows % divisor == 0))


def shards(occupied_green, empty_green, basis, time_weights):
    stacked = jnp.stack([occupied_green, empty_green])
    time_count = occupied_green.shape[0]
    coef_block = occupied_green.shape[1]
    row_total = basis.shape[0]
    scale_factor = 1.0 / NR

    def make_accumulate(combined_rows):

        def accumulate(running, basis_piece, first_row):
            piece_rows = basis_piece.shape[0]
            step_rows = step_size(piece_rows)

            def one_step(step_index, inner):
                basis_subpart = lax.dynamic_slice_in_dim(
                    basis_piece, step_index * step_rows, step_rows, 0
                )
                real_pair = jnp.einsum(
                    "qoa,ba->qob", combined_rows, basis_subpart, preferred_element_type=jnp.float32
                )
                product = (real_pair[0] * real_pair[1]).astype(jnp.bfloat16)
                return inner + jnp.dot(product, basis_subpart, preferred_element_type=jnp.float32)

            return lax.fori_loop(0, piece_rows // step_rows, one_step, running)

        return accumulate

    initial = jnp.zeros((time_count * row_total, NB), jnp.float32)
    projected = jnp.einsum(
        "sl,ftkl->ftsk",
        basis,
        lax.all_gather(stacked, "grid", axis=2, tiled=True),
        preferred_element_type=jnp.float32,
    ).astype(jnp.bfloat16)
    combined_rows = projected.reshape(2, time_count * row_total, NB)
    accumulate = make_accumulate(combined_rows)
    summed = accumulate(initial, lax.all_gather(basis, "grid", axis=0, tiled=True), jnp.int32(0))
    back_half = summed.astype(jnp.bfloat16).reshape(time_count, row_total, NB)
    coef_rows = lax.psum_scatter(
        jnp.einsum("tsk,sl->ktl", back_half, basis, preferred_element_type=jnp.float32).reshape(
            lax.axis_size("grid") * coef_block, time_count * NB
        ),
        "grid",
        scatter_dimension=0,
        tiled=True,
    ).reshape(coef_block, time_count, NB)
    block_list = [coef_rows[:, 0]]
    result = lax.psum_scatter(
        weigh_times(time_weights, block_list, scale_factor), "tm", scatter_dimension=0, tiled=True
    )
    return result


def solution(mesh):
    in_specs = (P("tm", "grid", None), P("tm", "grid", None), P("grid", None), P())
    out_specs = P("tm", "grid", None)
    return jax.shard_map(shards, mesh=mesh, in_specs=in_specs, out_specs=out_specs, check_vma=False)
```

profile of v0, /device:TPU:0, one launch (start us, length us, event | category | flops | bytes accessed | tf_op | source)
XLA Modules:
  0.0 431.6 jit_solution(16188916720244867342)
XLA Ops:
  6.5 1.7 pad_maximum_fusion
  8.3 0.7 all-gather.3.cloned.1.call-update
  9.1 53.6 %all-gather.5.cloned.1.call-done = bf16[2,1,1024,1024]{3,2,0,1:T(8,128)(2,1)} async-done(((bf16[2,1,64,1024]{3,2,0,1:T(8,128)(2,1)}), bf16[2,1,1024,1024]{3,2,0,1:T(8,128)(2,1)}) %all-gather.5.cloned.1.call-update) | async-done | bytes 4194320 | tf_op jit(solution)/shard_map/all_gather | solution.py:53
  62.7 7.9 %convert_bitcast_fusion = bf16[2,768,1024]{1,2,0:T(8,128)(2,1)} fusion(bf16[2,1,1024,1024]{3,2,0,1:T(8,128)(2,1)} %all-gather.5.cloned.1.call-done, bf16[768,1024]{1,0:T(8,128)(2,1)} %param.8), kind=kOutput, calls=%fused_computation.13 | convolution fusion | flops 3222798336 | bytes 8912896 | tf_op jit(solution)/shard_map/sl,ftkl->ftsk/dot_general | solution.py:50
  70.5 3.2 copy.5
  73.8 117.6 %all-gather.3.cloned.1.call-done = bf16[12288,1024]{1,0:T(8,128)(2,1)} async-done(((bf16[768,1024]{1,0:T(8,128)(2,1)}), bf16[12288,1024]{1,0:T(8,128)(2,1)}) %all-gather.3.cloned.1.call-update) | async-done | bytes 25165840 | tf_op jit(solution)/shard_map/all_gather | solution.py:58
  191.3 138.8 %while.14 = (s32[]{:T(128)}, f32[768,1024]{1,0:T(8,128)}, bf16[12288,1024]{1,0:T(8,128)(2,1)}, bf16[2,768,1024]{2,1,0:T(8,128)(2,1)S(1)}, s32[]{:T(128)}, /*index=5*/s32[]{:T(128)}, s32[]{:T(128)}, s32[]{:T(128)}) while((s32[]{:T(128)}, f32[768,1024]{1,0:T(8,128)}, bf16[12288,1024]{1,0:T(8,128)(2,1)}, ...), condition=%wide.region_1.0_spmd.clone, body=%wide.region_0.0_spmd.clone.sunk | while | flops 9668395008 | bytes 42991772 | solution.py:45
  191.4 11.5 %convolution_bitcast_fusion.2 = f32[2,768,2048]{1,2,0:T(8,128)} fusion(bf16[2,768,1024]{2,1,0:T(8,128)(2,1)S(1)} %get-tuple-element.156, bf16[12288,1024]{1,0:T(8,128)(2,1)} %get-tuple-element.155, s32[]{:T(128)S(6)} %select_n.13), kind=kOutput, calls=%fused_computation.2.clone.1 | convolution fusion | flops 6442450944 | bytes 19922948 | tf_op jit(solution)/shard_map/while/body/eval_jaxpr/qoa,ba->qob/dot_general | solution.py:39
  202.9 10.9 %select_add_fusion.2 = f32[768,1024]{1,0:T(8,128)} fusion(f32[768,1024]{1,0:T(8,128)} %get-tuple-element.146, bf16[12288,1024]{1,0:T(8,128)(2,1)} %get-tuple-element.155, s32[]{:T(128)S(6)} %select_n.13, f32[2,768,2048]{1,2,0:T(8,128)} %convolution_bitcast_fusion.2, pred[]{:T(512)S(6)} %compare.3), kind=kOutput, calls=%fused_computation.8.clone.1 | convolution fusion | flops 3225944064 | bytes 23068676 | tf_op jit(solution)/shard_map/while/body/eval_jaxpr/dot_general | solution.py:43
  213.7 11.5 %convolution_bitcast_fusion.2 = f32[2,768,2048]{1,2,0:T(8,128)} fusion(bf16[2,768,1024]{2,1,0:T(8,128)(2,1)S(1)} %get-tuple-element.156, bf16[12288,1024]{1,0:T(8,128)(2,1)} %get-tuple-element.155, s32[]{:T(128)S(6)} %select_n.13), kind=kOutput, calls=%fused_computation.2.clone.1 | convolution fusion | flops 6442450944 | bytes 19922948 | tf_op jit(solution)/shard_map/while/body/eval_jaxpr/qoa,ba->qob/dot_general | solution.py:39
  225.2 11.8 %select_add_fusion.2 = f32[768,1024]{1,0:T(8,128)} fusion(f32[768,1024]{1,0:T(8,128)} %get-tuple-element.146, bf16[12288,1024]{1,0:T(8,128)(2,1)} %get-tuple-element.155, s32[]{:T(128)S(6)} %select_n.13, f32[2,768,2048]{1,2,0:T(8,128)} %convolution_bitcast_fusion.2, pred[]{:T(512)S(6)} %compare.3), kind=kOutput, calls=%fused_computation.8.clone.1 | convolution fusion | flops 3225944064 | bytes 23068676 | tf_op jit(solution)/shard_map/while/body/eval_jaxpr/dot_general | solution.py:43
  237.0 11.5 %convolution_bitcast_fusion.2 = f32[2,768,2048]{1,2,0:T(8,128)} fusion(bf16[2,768,1024]{2,1,0:T(8,128)(2,1)S(1)} %get-tuple-element.156, bf16[12288,1024]{1,0:T(8,128)(2,1)} %get-tuple-element.155, s32[]{:T(128)S(6)} %select_n.13), kind=kOutput, calls=%fused_computation.2.clone.1 | convolution fusion | flops 6442450944 | bytes 19922948 | tf_op jit(solution)/shard_map/while/body/eval_jaxpr/qoa,ba->qob/dot_general | solution.py:39
  248.5 11.8 %select_add_fusion.2 = f32[768,1024]{1,0:T(8,128)} fusion(f32[768,1024]{1,0:T(8,128)} %get-tuple-element.146, bf16[12288,1024]{1,0:T(8,128)(2,1)} %get-tuple-element.155, s32[]{:T(128)S(6)} %select_n.13, f32[2,768,2048]{1,2,0:T(8,128)} %convolution_bitcast_fusion.2, pred[]{:T(512)S(6)} %compare.3), kind=kOutput, calls=%fused_computation.8.clone.1 | convolution fusion | flops 3225944064 | bytes 23068676 | tf_op jit(solution)/shard_map/while/body/eval_jaxpr/dot_general | solution.py:43
  260.3 11.5 %convolution_bitcast_fusion.2 = f32[2,768,2048]{1,2,0:T(8,128)} fusion(bf16[2,768,1024]{2,1,0:T(8,128)(2,1)S(1)} %get-tuple-element.156, bf16[12288,1024]{1,0:T(8,128)(2,1)} %get-tuple-element.155, s32[]{:T(128)S(6)} %select_n.13), kind=kOutput, calls=%fused_computation.2.clone.1 | convolution fusion | flops 6442450944 | bytes 19922948 | tf_op jit(solution)/shard_map/while/body/eval_jaxpr/qoa,ba->qob/dot_general | solution.py:39
  271.8 11.8 %select_add_fusion.2 = f32[768,1024]{1,0:T(8,128)} fusion(f32[768,1024]{1,0:T(8,128)} %get-tuple-element.146, bf16[12288,1024]{1,0:T(8,128)(2,1)} %get-tuple-element.155, s32[]{:T(128)S(6)} %select_n.13, f32[2,768,2048]{1,2,0:T(8,128)} %convolution_bitcast_fusion.2, pred[]{:T(512)S(6)} %compare.3), kind=kOutput, calls=%fused_computation.8.clone.1 | convolution fusion | flops 3225944064 | bytes 23068676 | tf_op jit(solution)/shard_map/while/body/eval_jaxpr/dot_general | solution.py:43
  283.6 11.5 %convolution_bitcast_fusion.2 = f32[2,768,2048]{1,2,0:T(8,128)} fusion(bf16[2,768,1024]{2,1,0:T(8,128)(2,1)S(1)} %get-tuple-element.156, bf16[12288,1024]{1,0:T(8,128)(2,1)} %get-tuple-element.155, s32[]{:T(128)S(6)} %select_n.13), kind=kOutput, calls=%fused_computation.2.clone.1 | convolution fusion | flops 6442450944 | bytes 19922948 | tf_op jit(solution)/shard_map/while/body/eval_jaxpr/qoa,ba->qob/dot_general | solution.py:39
  295.1 11.8 %select_add_fusion.2 = f32[768,1024]{1,0:T(8,128)} fusion(f32[768,1024]{1,0:T(8,128)} %get-tuple-element.146, bf16[12288,1024]{1,0:T(8,128)(2,1)} %get-tuple-element.155, s32[]{:T(128)S(6)} %select_n.13, f32[2,768,2048]{1,2,0:T(8,128)} %convolution_bitcast_fusion.2, pred[]{:T(512)S(6)} %compare.3), kind=kOutput, calls=%fused_computation.8.clone.1 | convolution fusion | flops 3225944064 | bytes 23068676 | tf_op jit(solution)/shard_map/while/body/eval_jaxpr/dot_general | solution.py:43
  306.9 11.5 %convolution_bitcast_fusion.2 = f32[2,768,2048]{1,2,0:T(8,128)} fusion(bf16[2,768,1024]{2,1,0:T(8,128)(2,1)S(1)} %get-tuple-element.156, bf16[12288,1024]{1,0:T(8,128)(2,1)} %get-tuple-element.155, s32[]{:T(128)S(6)} %select_n.13), kind=kOutput, calls=%fused_computation.2.clone.1 | convolution fusion | flops 6442450944 | bytes 19922948 | tf_op jit(solution)/shard_map/while/body/eval_jaxpr/qoa,ba->qob/dot_general | solution.py:39
  318.4 11.8 %select_add_fusion.2 = f32[768,1024]{1,0:T(8,128)} fusion(f32[768,1024]{1,0:T(8,128)} %get-tuple-element.146, bf16[12288,1024]{1,0:T(8,128)(2,1)} %get-tuple-element.155, s32[]{:T(128)S(6)} %select_n.13, f32[2,768,2048]{1,2,0:T(8,128)} %convolution_bitcast_fusion.2, pred[]{:T(512)S(6)} %compare.3), kind=kOutput, calls=%fused_computation.8.clone.1 | convolution fusion | flops 3225944064 | bytes 23068676 | tf_op jit(solution)/shard_map/while/body/eval_jaxpr/dot_general | solution.py:43
  330.2 6.1 %fusion.18 = f32[1024,1024]{1,0:T(8,128)} fusion(bf16[768,1024]{1,0:T(8,128)(2,1)} %param.8, f32[768,1024]{1,0:T(8,128)} %get-tuple-element.84), kind=kOutput, calls=%fused_computation.15 | convolution fusion | flops 1611399168 | bytes 8912896 | tf_op jit(solution)/shard_map/tsk,sl->ktl/dot_general | solution.py:61
  336.4 0.2 dynamic-slice_reduce_fusion
  336.6 72.7 %reduce-scatter.3.cloned.1.call-done = f32[64,1024]{1,0:T(8,128)} async-done(((f32[1024,1024]{1,0:T(8,128)}), f32[64,1024]{1,0:T(8,128)}) %reduce-scatter.3.cloned.1.call-update) | async-done | bytes 262160 | tf_op jit(solution)/shard_map/reduce_scatter | solution.py:60
  409.2 1.9 multiply_multiply_fusion
  411.1 13.9 %reduce-scatter.5.cloned.1.call-done = f32[1,64,1024]{2,1,0:T(8,128)} async-done(((f32[2,64,1024]{2,1,0:T(8,128)}), f32[1,64,1024]{2,1,0:T(8,128)}) %reduce-scatter.5.cloned.1.call-update) | async-done | bytes 262160 | tf_op jit(solution)/shard_map/reduce_scatter | solution.py:69
  (10 shorter events, 0.2 us)
Async XLA Ops:
  6.5 329.8 %copy-start = (f32[2,2]{1,0:T(2,128)S(1)}, f32[2,2]{1,0:T(2,128)}, u32[]{:S(2)}) copy-start(f32[2,2]{1,0:T(2,128)} %param.9) | copy-start | bytes 52
  6.5 56.1 %all-gather.5.cloned.1.call-start = ((), (), s32[]{:S(2)}) async-start(), calls=%async_computation.3 | async-start | bytes 4456448 | tf_op jit(solution)/shard_map/all_gather | solution.py:53
  8.3 183.1 %all-gather.3.cloned.1.call-start = ((), (), s32[]{:S(2)}) async-start(), calls=%async_computation.2 | async-start | bytes 26738688 | tf_op jit(solution)/shard_map/all_gather | solution.py:58
  9.0 400.2 %reduce-scatter.3.cloned.1.call-start = ((), (), s32[]{:S(2)}) async-start(), calls=%async_computation.4 | async-start | bytes 4456448 | tf_op jit(solution)/shard_map/reduce_scatter | solution.py:60
  336.3 88.8 %reduce-scatter.5.cloned.1.call-start = ((), (), s32[]{:S(2)}) async-start(), calls=%async_computation.5 | async-start | bytes 786432 | tf_op jit(solution)/shard_map/reduce_scatter | solution.py:69
Sparse Core Ops, SparseCore 0:
  9.5 53.1 all-gather.4
  64.3 127.0 all-gather.2
  336.4 72.7 reduce-scatter.2
  411.3 13.6 reduce-scatter.4
where the time goes:
time: 432 us
  waiting for transfers between devices  259 us (60%)
  matrix products  153 us (35%)
  between operations  13.2 us (3%)
    all_gather x1, waiting for transfers between devices, shards(): lax.all_gather(basis, 'grid', axis=0, tiled=True)  118 us
    reduce_scatter x1, waiting for transfers between devices, shards(): lax.psum_scatter(jnp.einsum('tsk,sl->ktl', back_half, basis, preferred_el...  72.7 us
    dot_general x6, matrix products, one_step(): jnp.dot(product, basis_subpart, preferred_element_type=jnp.float32)  69.8 us
    dot_general x6, matrix products, one_step(): jnp.einsum('qoa,ba->qob', combined_rows, basis_subpart, preferred_element...  69 us
    all_gather x1, waiting for transfers between devices, shards(): lax.all_gather(stacked, 'grid', axis=2, tiled=True)  53.6 us
    reduce_scatter x1, waiting for transfers between devices, shards(): lax.psum_scatter(weigh_times(time_weights, block_list, scale_factor), 'tm...  13.9 us
  transfers between devices with their start and end apart: 4, of which 4 were waited for; matrix products, arithmetic and copies ran while one was open for 3% of the time, Pallas kernels for 0%

commit v1 on v0

--- a/solution.py
+++ b/solution.py
@@ -1,3 +1,4 @@
+import functools
 import jax
 import jax.numpy as jnp
 from jax import lax
@@ -5,6 +6,39 @@
 
 NR = 12288
 NB = 1024
+
+
+def answer_pages_on(patch, on_dim):
+    met_up = list(patch.shape[1:])
+    met_up[on_dim] *= patch.shape[0]
+    w1 = jnp.moveaxis(patch, 0, on_dim).reshape(met_up)
+    return w1
+
+
+def save_the_stocks(payload, which_axis, dim_at):
+    n_parts = lax.axis_size(which_axis)
+    local_next = range(n_parts)
+    z1 = map(lambda hop_no: (hop_no, (hop_no + 1) % n_parts), local_next)
+    so_far_all = list(z1)
+    copies = [(i, nth) for nth, i in so_far_all]
+    a_next, s_next = ([], [])
+    for b in range(n_parts - 1):
+        if b % 2 == 0:
+            new = lax.ppermute(a_next[-1] if a_next else payload, which_axis, so_far_all)
+            a_next.append(new)
+        else:
+            fresh = lax.ppermute(s_next[-1] if s_next else payload, which_axis, copies)
+            s_next.append(fresh)
+    wide_out = jnp.stack([*a_next[::-1], payload, *s_next])
+    r_now = lax.axis_index(which_axis)
+    part_next = len(a_next)
+    side_arr = r_now - part_next
+    wide_out = wide_out[(jnp.arange(n_parts) - side_arr) % n_parts]
+    back = answer_pages_on(wide_out, dim_at)
+    return back
+
+
+_supply_all_patch = functools.partial(save_the_stocks, which_axis="grid", dim_at=0)
 
 
 def weigh_times(time_weights, block_list, scale_factor):
@@ -55,7 +89,7 @@
     ).astype(jnp.bfloat16)
     combined_rows = projected.reshape(2, time_count * row_total, NB)
     accumulate = make_accumulate(combined_rows)
-    summed = accumulate(initial, lax.all_gather(basis, "grid", axis=0, tiled=True), jnp.int32(0))
+    summed = accumulate(initial, _supply_all_patch(basis), jnp.int32(0))
     back_half = summed.astype(jnp.bfloat16).reshape(time_count, row_total, NB)
     coef_rows = lax.psum_scatter(
         jnp.einsum("tsk,sl->ktl", back_half, basis, preferred_element_type=jnp.float32).reshape(

time: 432 us -> 587 us (1.36)
  starting transfers between devices: 0.12 us -> 177 us
  waiting for transfers between devices: 259 us -> 185 us
  local copies, waits for them, and re-layouts: 3.4 us -> 54.3 us
    ppermute x0 -> x15, starting transfers between devices: none -> 177 us  [the longest x8 173 us: save_the_stocks(): lax.ppermute(a_next[-1] if a_next else payload, which_axis, so_far_all)]
    all_gather x1 -> x0, waiting for transfers between devices: 118 us -> none  [shards(): lax.all_gather(basis, 'grid', axis=0, tiled=True)]
    ppermute x0 -> x15, waiting for transfers between devices: none -> 71.8 us  [the longest x8 71.8 us: save_the_stocks(): lax.ppermute(a_next[-1] if a_next else payload, which_axis, so_far_all)]
    all_gather x1, waiting for transfers between devices: 53.6 us -> 0.02 us  [shards(): lax.all_gather(stacked, 'grid', axis=2, tiled=True)]
    unnamed x3 -> x56, local copies, waits for them, and re-layouts: 3.21 us -> 34.6 us
    reduce_scatter x1, waiting for transfers between devices: 72.7 us -> 99.4 us  [shards(): lax.psum_scatter(jnp.einsum('tsk,sl->ktl', back_half, basis, preferred_el...]
    gather x0 -> x1, local copies, waits for them, and re-layouts: none -> 18.2 us  [save_the_stocks(): wide_out = wide_out[(jnp.arange(n_parts) - side_arr) % n_parts]]
  transfers between devices with their start and end apart: 4 -> 18, of which waited for: 4 -> 9; matrix products, arithmetic and copies ran while one was open for 3% -> 7% of each run, Pallas kernels for 0% -> 0%
where the time goes in v1:
time: 587 us
  waiting for transfers between devices  185 us (32%)
  starting transfers between devices  177 us (30%)
  matrix products  153 us (26%)
  local copies, waits for them, and re-layouts  54.3 us (9%)
  between operations  13.3 us (2%)
    ppermute x8, starting transfers between devices, save_the_stocks(): lax.ppermute(a_next[-1] if a_next else payload, which_axis, so_far_all)  173 us
    reduce_scatter x1, waiting for transfers between devices, shards(): lax.psum_scatter(jnp.einsum('tsk,sl->ktl', back_half, basis, preferred_el...  99.4 us
    ppermute x8, waiting for transfers between devices, save_the_stocks(): lax.ppermute(a_next[-1] if a_next else payload, which_axis, so_far_all)  71.8 us
    dot_general x6, matrix products, one_step(): jnp.dot(product, basis_subpart, preferred_element_type=jnp.float32)  69.9 us
    dot_general x6, matrix products, one_step(): jnp.einsum('qoa,ba->qob', combined_rows, basis_subpart, preferred_element...  68.8 us
    unnamed x56, local copies, waits for them, and re-layouts  34.6 us
    gather x1, local copies, waits for them, and re-layouts, save_the_stocks(): wide_out = wide_out[(jnp.arange(n_parts) - side_arr) % n_parts]  18.2 us
    reduce_scatter x1, waiting for transfers between devices, shards(): lax.psum_scatter(weigh_times(time_weights, block_list, scale_factor), 'tm...  14.1 us
  transfers between devices with their start and end apart: 18, of which 9 were waited for; matrix products, arithmetic and copies ran while one was open for 7% of the time, Pallas kernels for 0%

profile of v1, /device:TPU:0, one launch (start us, length us, event | category | flops | bytes accessed | tf_op | source)
XLA Modules:
  0.0 586.8 jit_solution(5886556723408446443)
XLA Ops:
  7.0 23.3 %collective-permute-done = bf16[768,1024]{1,0:T(8,128)(2,1)S(1)} collective-permute-done((bf16[768,1024]{1,0:T(8,128)(2,1)}, bf16[768,1024]{1,0:T(8,128)(2,1)S(1)}, u32[]{:S(2)}, u32[]{:S(2)}) %collective-permute-start) | collective-permute-done | bytes 1572896 | tf_op jit(solution)/shard_map/ppermute | solution.py:27
  35.9 18.2 %collective-permute-done.1 = bf16[768,1024]{1,0:T(8,128)(2,1)S(1)} collective-permute-done((bf16[768,1024]{1,0:T(8,128)(2,1)S(1)}, bf16[768,1024]{1,0:T(8,128)(2,1)S(1)}, u32[]{:S(2)}, u32[]{:S(2)}) %collective-permute-start.1) | collective-permute-done | bytes 1572896 | tf_op jit(solution)/shard_map/ppermute | solution.py:27
  54.1 11.0 %collective-permute-start.2 = (bf16[768,1024]{1,0:T(8,128)(2,1)S(1)}, bf16[768,1024]{1,0:T(8,128)(2,1)}, u32[]{:S(2)}, u32[]{:S(2)}) collective-permute-start(bf16[768,1024]{1,0:T(8,128)(2,1)S(1)} %collective-permute-done.1), channel_id=1, source_target_pairs={{0,1},{1,2},{2,3},{3,4},{4,5},{5,6},{6,7},{7,8},{8,9},{9,10},{10,1... | collective-permute-start | bytes 4718600 | tf_op jit(solution)/shard_map/ppermute | solution.py:27
  76.9 27.7 %collective-permute-start.3 = (bf16[768,1024]{1,0:T(8,128)(2,1)}, bf16[768,1024]{1,0:T(8,128)(2,1)S(1)}, u32[]{:S(2)}, u32[]{:S(2)}) collective-permute-start(bf16[768,1024]{1,0:T(8,128)(2,1)} %collective-permute-done.2), channel_id=1, source_target_pairs={{0,1},{1,2},{2,3},{3,4},{4,5},{5,6},{6,7},{7,8},{8,9},{9,10},{10,1... | collective-permute-start | bytes 4718600 | tf_op jit(solution)/shard_map/ppermute | solution.py:27
  111.3 41.6 %collective-permute-start.4 = (bf16[768,1024]{1,0:T(8,128)(2,1)S(1)}, bf16[768,1024]{1,0:T(8,128)(2,1)S(1)}, u32[]{:S(2)}, u32[]{:S(2)}) collective-permute-start(bf16[768,1024]{1,0:T(8,128)(2,1)S(1)} %collective-permute-done.3), channel_id=1, source_target_pairs={{0,1},{1,2},{2,3},{3,4},{4,5},{5,6},{6,7},{7,8},{8,9},{9,10},{10,1... | collective-permute-start | bytes 4718600 | tf_op jit(solution)/shard_map/ppermute | solution.py:27
  163.8 25.7 %collective-permute-start.5 = (bf16[768,1024]{1,0:T(8,128)(2,1)S(1)}, bf16[768,1024]{1,0:T(8,128)(2,1)S(1)}, u32[]{:S(2)}, u32[]{:S(2)}) collective-permute-start(bf16[768,1024]{1,0:T(8,128)(2,1)S(1)} %collective-permute-done.4), channel_id=1, source_target_pairs={{0,1},{1,2},{2,3},{3,4},{4,5},{5,6},{6,7},{7,8},{8,9},{9,10},{10,1... | collective-permute-start | bytes 4718600 | tf_op jit(solution)/shard_map/ppermute | solution.py:27
  192.6 33.7 %collective-permute-start.6 = (bf16[768,1024]{1,0:T(8,128)(2,1)S(1)}, bf16[768,1024]{1,0:T(8,128)(2,1)}, u32[]{:S(2)}, u32[]{:S(2)}) collective-permute-start(bf16[768,1024]{1,0:T(8,128)(2,1)S(1)} %collective-permute-done.5), channel_id=1, source_target_pairs={{0,1},{1,2},{2,3},{3,4},{4,5},{5,6},{6,7},{7,8},{8,9},{9,10},{10,1... | collective-permute-start | bytes 4718600 | tf_op jit(solution)/shard_map/ppermute | solution.py:27
  229.4 32.5 %collective-permute-start.7 = (bf16[768,1024]{1,0:T(8,128)(2,1)}, bf16[768,1024]{1,0:T(8,128)(2,1)}, u32[]{:S(2)}, u32[]{:S(2)}) collective-permute-start(bf16[768,1024]{1,0:T(8,128)(2,1)} %collective-permute-done.6), channel_id=1, source_target_pairs={{0,1},{1,2},{2,3},{3,4},{4,5},{5,6},{6,7},{7,8},{8,9},{9,10},{10,1... | collective-permute-start | bytes 4718600 | tf_op jit(solution)/shard_map/ppermute | solution.py:27
  301.5 18.2 %gather_fusion = bf16[16,768,1024]{2,1,0:T(8,128)(2,1)} fusion(bf16[16,768,1024]{2,1,0:T(8,128)(2,1)} %bitcast_dynamic-update-slice_fusion, s32[1024]{0:T(1024)S(1)} %pad_clamp_fusion), kind=kCustom, calls=%fused_computation | custom fusion | bytes 50331712 | tf_op jit(solution)/shard_map/gather | solution.py:36
  319.8 138.7 %while.14 = (s32[]{:T(128)}, f32[768,1024]{1,0:T(8,128)}, bf16[12288,1024]{1,0:T(8,128)(2,1)}, bf16[2,768,1024]{2,1,0:T(8,128)(2,1)S(1)}, s32[]{:T(128)}, /*index=5*/s32[]{:T(128)}, s32[]{:T(128)}, s32[]{:T(128)}) while((s32[]{:T(128)}, f32[768,1024]{1,0:T(8,128)}, bf16[12288,1024]{1,0:T(8,128)(2,1)}, ...), condition=%wide.region_1.2_spmd.clone, body=%wide.region_0.1_spmd.clone.sunk | while | flops 9668395008 | bytes 42991764 | solution.py:79
  319.8 11.5 %convolution_bitcast_fusion.2 = f32[2,768,2048]{1,2,0:T(8,128)} fusion(bf16[2,768,1024]{2,1,0:T(8,128)(2,1)S(1)} %get-tuple-element.156, bf16[12288,1024]{1,0:T(8,128)(2,1)} %get-tuple-element.155, s32[]{:T(128)S(6)} %select_n.47), kind=kOutput, calls=%fused_computation.3.clone.1 | convolution fusion | flops 6442450944 | bytes 19922948 | tf_op jit(solution)/shard_map/while/body/eval_jaxpr/qoa,ba->qob/dot_general | solution.py:73
  331.2 10.9 %select_add_fusion.2 = f32[768,1024]{1,0:T(8,128)} fusion(f32[768,1024]{1,0:T(8,128)} %get-tuple-element.146, bf16[12288,1024]{1,0:T(8,128)(2,1)} %get-tuple-element.155, s32[]{:T(128)S(6)} %select_n.47, f32[2,768,2048]{1,2,0:T(8,128)} %convolution_bitcast_fusion.2, pred[]{:T(512)S(6)} %compare.10), kind=kOutput, calls=%fused_computation.9.clone.1 | convolution fusion | flops 3225944064 | bytes 23068676 | tf_op jit(solution)/shard_map/while/body/eval_jaxpr/dot_general | solution.py:77
  342.2 11.5 %convolution_bitcast_fusion.2 = f32[2,768,2048]{1,2,0:T(8,128)} fusion(bf16[2,768,1024]{2,1,0:T(8,128)(2,1)S(1)} %get-tuple-element.156, bf16[12288,1024]{1,0:T(8,128)(2,1)} %get-tuple-element.155, s32[]{:T(128)S(6)} %select_n.47), kind=kOutput, calls=%fused_computation.3.clone.1 | convolution fusion | flops 6442450944 | bytes 19922948 | tf_op jit(solution)/shard_map/while/body/eval_jaxpr/qoa,ba->qob/dot_general | solution.py:73
  353.6 11.8 %select_add_fusion.2 = f32[768,1024]{1,0:T(8,128)} fusion(f32[768,1024]{1,0:T(8,128)} %get-tuple-element.146, bf16[12288,1024]{1,0:T(8,128)(2,1)} %get-tuple-element.155, s32[]{:T(128)S(6)} %select_n.47, f32[2,768,2048]{1,2,0:T(8,128)} %convolution_bitcast_fusion.2, pred[]{:T(512)S(6)} %compare.10), kind=kOutput, calls=%fused_computation.9.clone.1 | convolution fusion | flops 3225944064 | bytes 23068676 | tf_op jit(solution)/shard_map/while/body/eval_jaxpr/dot_general | solution.py:77
  365.4 11.5 %convolution_bitcast_fusion.2 = f32[2,768,2048]{1,2,0:T(8,128)} fusion(bf16[2,768,1024]{2,1,0:T(8,128)(2,1)S(1)} %get-tuple-element.156, bf16[12288,1024]{1,0:T(8,128)(2,1)} %get-tuple-element.155, s32[]{:T(128)S(6)} %select_n.47), kind=kOutput, calls=%fused_computation.3.clone.1 | convolution fusion | flops 6442450944 | bytes 19922948 | tf_op jit(solution)/shard_map/while/body/eval_jaxpr/qoa,ba->qob/dot_general | solution.py:73
  376.9 11.8 %select_add_fusion.2 = f32[768,1024]{1,0:T(8,128)} fusion(f32[768,1024]{1,0:T(8,128)} %get-tuple-element.146, bf16[12288,1024]{1,0:T(8,128)(2,1)} %get-tuple-element.155, s32[]{:T(128)S(6)} %select_n.47, f32[2,768,2048]{1,2,0:T(8,128)} %convolution_bitcast_fusion.2, pred[]{:T(512)S(6)} %compare.10), kind=kOutput, calls=%fused_computation.9.clone.1 | convolution fusion | flops 3225944064 | bytes 23068676 | tf_op jit(solution)/shard_map/while/body/eval_jaxpr/dot_general | solution.py:77
  388.7 11.5 %convolution_bitcast_fusion.2 = f32[2,768,2048]{1,2,0:T(8,128)} fusion(bf16[2,768,1024]{2,1,0:T(8,128)(2,1)S(1)} %get-tuple-element.156, bf16[12288,1024]{1,0:T(8,128)(2,1)} %get-tuple-element.155, s32[]{:T(128)S(6)} %select_n.47), kind=kOutput, calls=%fused_computation.3.clone.1 | convolution fusion | flops 6442450944 | bytes 19922948 | tf_op jit(solution)/shard_map/while/body/eval_jaxpr/qoa,ba->qob/dot_general | solution.py:73
  400.2 11.8 %select_add_fusion.2 = f32[768,1024]{1,0:T(8,128)} fusion(f32[768,1024]{1,0:T(8,128)} %get-tuple-element.146, bf16[12288,1024]{1,0:T(8,128)(2,1)} %get-tuple-element.155, s32[]{:T(128)S(6)} %select_n.47, f32[2,768,2048]{1,2,0:T(8,128)} %convolution_bitcast_fusion.2, pred[]{:T(512)S(6)} %compare.10), kind=kOutput, calls=%fused_computation.9.clone.1 | convolution fusion | flops 3225944064 | bytes 23068676 | tf_op jit(solution)/shard_map/while/body/eval_jaxpr/dot_general | solution.py:77
  412.0 11.5 %convolution_bitcast_fusion.2 = f32[2,768,2048]{1,2,0:T(8,128)} fusion(bf16[2,768,1024]{2,1,0:T(8,128)(2,1)S(1)} %get-tuple-element.156, bf16[12288,1024]{1,0:T(8,128)(2,1)} %get-tuple-element.155, s32[]{:T(128)S(6)} %select_n.47), kind=kOutput, calls=%fused_computation.3.clone.1 | convolution fusion | flops 6442450944 | bytes 19922948 | tf_op jit(solution)/shard_map/while/body/eval_jaxpr/qoa,ba->qob/dot_general | solution.py:73
  423.4 11.8 %select_add_fusion.2 = f32[768,1024]{1,0:T(8,128)} fusion(f32[768,1024]{1,0:T(8,128)} %get-tuple-element.146, bf16[12288,1024]{1,0:T(8,128)(2,1)} %get-tuple-element.155, s32[]{:T(128)S(6)} %select_n.47, f32[2,768,2048]{1,2,0:T(8,128)} %convolution_bitcast_fusion.2, pred[]{:T(512)S(6)} %compare.10), kind=kOutput, calls=%fused_computation.9.clone.1 | convolution fusion | flops 3225944064 | bytes 23068676 | tf_op jit(solution)/shard_map/while/body/eval_jaxpr/dot_general | solution.py:77
  435.2 11.5 %convolution_bitcast_fusion.2 = f32[2,768,2048]{1,2,0:T(8,128)} fusion(bf16[2,768,1024]{2,1,0:T(8,128)(2,1)S(1)} %get-tuple-element.156, bf16[12288,1024]{1,0:T(8,128)(2,1)} %get-tuple-element.155, s32[]{:T(128)S(6)} %select_n.47), kind=kOutput, calls=%fused_computation.3.clone.1 | convolution fusion | flops 6442450944 | bytes 19922948 | tf_op jit(solution)/shard_map/while/body/eval_jaxpr/qoa,ba->qob/dot_general | solution.py:73
  446.7 11.8 %select_add_fusion.2 = f32[768,1024]{1,0:T(8,128)} fusion(f32[768,1024]{1,0:T(8,128)} %get-tuple-element.146, bf16[12288,1024]{1,0:T(8,128)(2,1)} %get-tuple-element.155, s32[]{:T(128)S(6)} %select_n.47, f32[2,768,2048]{1,2,0:T(8,128)} %convolution_bitcast_fusion.2, pred[]{:T(512)S(6)} %compare.10), kind=kOutput, calls=%fused_computation.9.clone.1 | convolution fusion | flops 3225944064 | bytes 23068676 | tf_op jit(solution)/shard_map/while/body/eval_jaxpr/dot_general | solution.py:77
  464.9 99.4 %reduce-scatter.3.cloned.1.call-done = f32[64,1024]{1,0:T(8,128)} async-done(((f32[1024,1024]{1,0:T(8,128)}), f32[64,1024]{1,0:T(8,128)}) %reduce-scatter.3.cloned.1.call-update) | async-done | bytes 262160 | tf_op jit(solution)/shard_map/reduce_scatter | solution.py:94
  566.2 14.1 %reduce-scatter.5.cloned.1.call-done = f32[1,64,1024]{2,1,0:T(8,128)} async-done(((f32[2,64,1024]{2,1,0:T(8,128)}), f32[1,64,1024]{2,1,0:T(8,128)}) %reduce-scatter.5.cloned.1.call-update) | async-done | bytes 262160 | tf_op jit(solution)/shard_map/reduce_scatter | solution.py:103
  (94 shorter events, 89.5 us)
Async XLA Ops:
  6.5 458.2 %copy-start = (f32[2,2]{1,0:T(2,128)S(1)}, f32[2,2]{1,0:T(2,128)}, u32[]{:S(2)}) copy-start(f32[2,2]{1,0:T(2,128)} %param.9) | copy-start | bytes 52
  6.5 255.4 %all-gather.2.cloned.1.call-start = ((), (), s32[]{:S(2)}) async-start(), calls=%async_computation.2 | async-start | bytes 4456448 | tf_op jit(solution)/shard_map/all_gather | solution.py:87
  6.5 23.8 %collective-permute-start = (bf16[768,1024]{1,0:T(8,128)(2,1)}, bf16[768,1024]{1,0:T(8,128)(2,1)S(1)}, u32[]{:S(2)}, u32[]{:S(2)}) collective-permute-start(bf16[768,1024]{1,0:T(8,128)(2,1)} %param.8), channel_id=1, source_target_pairs={{0,1},{1,2},{2,3},{3,4},{4,5},{5,6},{6,7},{7,8},{8,9},{9,10},{10,1... | collective-permute-start | bytes 4718600 | tf_op jit(solution)/shard_map/ppermute | solution.py:27
  31.5 22.6 %collective-permute-start.1 = (bf16[768,1024]{1,0:T(8,128)(2,1)S(1)}, bf16[768,1024]{1,0:T(8,128)(2,1)S(1)}, u32[]{:S(2)}, u32[]{:S(2)}) collective-permute-start(bf16[768,1024]{1,0:T(8,128)(2,1)S(1)} %collective-permute-done), channel_id=1, source_target_pairs={{0,1},{1,2},{2,3},{3,4},{4,5},{5,6},{6,7},{7,8},{8,9},{9,10},{10,1... | collective-permute-start | bytes 4718600 | tf_op jit(solution)/shard_map/ppermute | solution.py:27
  31.5 35.4 %collective-permute-start.8 = (bf16[768,1024]{1,0:T(8,128)(2,1)}, bf16[768,1024]{1,0:T(8,128)(2,1)S(1)}, u32[]{:S(2)}, u32[]{:S(2)}) collective-permute-start(bf16[768,1024]{1,0:T(8,128)(2,1)} %param.8), channel_id=1, source_target_pairs={{1,0},{2,1},{3,2},{4,3},{5,4},{6,5},{7,6},{8,7},{9,8},{10,9},{11,1... | collective-permute-start | bytes 4718600 | tf_op jit(solution)/shard_map/ppermute | solution.py:30
  54.1 207.8 %copy-start.6 = (bf16[768,1024]{1,0:T(8,128)(2,1)}, bf16[768,1024]{1,0:T(8,128)(2,1)S(1)}, u32[]{:S(2)}) copy-start(bf16[768,1024]{1,0:T(8,128)(2,1)S(1)} %collective-permute-done.1) | copy-start | bytes 4718596
  54.1 22.7 %collective-permute-start.2 = (bf16[768,1024]{1,0:T(8,128)(2,1)S(1)}, bf16[768,1024]{1,0:T(8,128)(2,1)}, u32[]{:S(2)}, u32[]{:S(2)}) collective-permute-start(bf16[768,1024]{1,0:T(8,128)(2,1)S(1)} %collective-permute-done.1), channel_id=1, source_target_pairs={{0,1},{1,2},{2,3},{3,4},{4,5},{5,6},{6,7},{7,8},{8,9},{9,10},{10,1... | collective-permute-start | bytes 4718600 | tf_op jit(solution)/shard_map/ppermute | solution.py:27
  66.8 497.5 %reduce-scatter.3.cloned.1.call-start = ((), (), s32[]{:S(2)}) async-start(), calls=%async_computation.3 | async-start | bytes 4456448 | tf_op jit(solution)/shard_map/reduce_scatter | solution.py:94
  66.8 195.1 %copy-start.4 = (bf16[768,1024]{1,0:T(8,128)(2,1)}, bf16[768,1024]{1,0:T(8,128)(2,1)S(1)}, u32[]{:S(2)}) copy-start(bf16[768,1024]{1,0:T(8,128)(2,1)S(1)} %collective-permute-done.8) | copy-start | bytes 4718596
  66.9 37.7 %collective-permute-start.9 = (bf16[768,1024]{1,0:T(8,128)(2,1)S(1)}, bf16[768,1024]{1,0:T(8,128)(2,1)S(1)}, u32[]{:S(2)}, u32[]{:S(2)}) collective-permute-start(bf16[768,1024]{1,0:T(8,128)(2,1)S(1)} %collective-permute-done.8), channel_id=1, source_target_pairs={{1,0},{2,1},{3,2},{4,3},{5,4},{6,5},{7,6},{8,7},{9,8},{10,9},{11,1... | collective-permute-start | bytes 4718600 | tf_op jit(solution)/shard_map/ppermute | solution.py:30
  76.9 34.5 %collective-permute-start.3 = (bf16[768,1024]{1,0:T(8,128)(2,1)}, bf16[768,1024]{1,0:T(8,128)(2,1)S(1)}, u32[]{:S(2)}, u32[]{:S(2)}) collective-permute-start(bf16[768,1024]{1,0:T(8,128)(2,1)} %collective-permute-done.2), channel_id=1, source_target_pairs={{0,1},{1,2},{2,3},{3,4},{4,5},{5,6},{6,7},{7,8},{8,9},{9,10},{10,1... | collective-permute-start | bytes 4718600 | tf_op jit(solution)/shard_map/ppermute | solution.py:27
  105.7 47.2 %collective-permute-start.10 = (bf16[768,1024]{1,0:T(8,128)(2,1)S(1)}, bf16[768,1024]{1,0:T(8,128)(2,1)S(1)}, u32[]{:S(2)}, u32[]{:S(2)}) collective-permute-start(bf16[768,1024]{1,0:T(8,128)(2,1)S(1)} %collective-permute-done.9), channel_id=1, source_target_pairs={{1,0},{2,1},{3,2},{4,3},{5,4},{6,5},{7,6},{8,7},{9,8},{10,9},{11,1... | collective-permute-start | bytes 4718600 | tf_op jit(solution)/shard_map/ppermute | solution.py:30
  111.3 114.9 %copy-start.14 = (bf16[768,1024]{1,0:T(8,128)(2,1)}, bf16[768,1024]{1,0:T(8,128)(2,1)S(1)}, u32[]{:S(2)}) copy-start(bf16[768,1024]{1,0:T(8,128)(2,1)S(1)} %collective-permute-done.3) | copy-start | bytes 4718596
  111.3 52.5 %collective-permute-start.4 = (bf16[768,1024]{1,0:T(8,128)(2,1)S(1)}, bf16[768,1024]{1,0:T(8,128)(2,1)S(1)}, u32[]{:S(2)}, u32[]{:S(2)}) collective-permute-start(bf16[768,1024]{1,0:T(8,128)(2,1)S(1)} %collective-permute-done.3), channel_id=1, source_target_pairs={{0,1},{1,2},{2,3},{3,4},{4,5},{5,6},{6,7},{7,8},{8,9},{9,10},{10,1... | collective-permute-start | bytes 4718600 | tf_op jit(solution)/shard_map/ppermute | solution.py:27
  154.1 35.5 %collective-permute-start.11 = (bf16[768,1024]{1,0:T(8,128)(2,1)S(1)}, bf16[768,1024]{1,0:T(8,128)(2,1)S(1)}, u32[]{:S(2)}, u32[]{:S(2)}) collective-permute-start(bf16[768,1024]{1,0:T(8,128)(2,1)S(1)} %collective-permute-done.10), channel_id=1, source_target_pairs={{1,0},{2,1},{3,2},{4,3},{5,4},{6,5},{7,6},{8,7},{9,8},{10,9},{11,1... | collective-permute-start | bytes 4718600 | tf_op jit(solution)/shard_map/ppermute | solution.py:30
  163.8 62.4 %copy-start.16 = (bf16[768,1024]{1,0:T(8,128)(2,1)}, bf16[768,1024]{1,0:T(8,128)(2,1)S(1)}, u32[]{:S(2)}) copy-start(bf16[768,1024]{1,0:T(8,128)(2,1)S(1)} %collective-permute-done.4) | copy-start | bytes 4718596
  163.8 28.8 %collective-permute-start.5 = (bf16[768,1024]{1,0:T(8,128)(2,1)S(1)}, bf16[768,1024]{1,0:T(8,128)(2,1)S(1)}, u32[]{:S(2)}, u32[]{:S(2)}) collective-permute-start(bf16[768,1024]{1,0:T(8,128)(2,1)S(1)} %collective-permute-done.4), channel_id=1, source_target_pairs={{0,1},{1,2},{2,3},{3,4},{4,5},{5,6},{6,7},{7,8},{8,9},{9,10},{10,1... | collective-permute-start | bytes 4718600 | tf_op jit(solution)/shard_map/ppermute | solution.py:27
  190.7 35.5 %collective-permute-start.12 = (bf16[768,1024]{1,0:T(8,128)(2,1)S(1)}, bf16[768,1024]{1,0:T(8,128)(2,1)}, u32[]{:S(2)}, u32[]{:S(2)}) collective-permute-start(bf16[768,1024]{1,0:T(8,128)(2,1)S(1)} %collective-permute-done.11), channel_id=1, source_target_pairs={{1,0},{2,1},{3,2},{4,3},{5,4},{6,5},{7,6},{8,7},{9,8},{10,9},{11,1... | collective-permute-start | bytes 4718600 | tf_op jit(solution)/shard_map/ppermute | solution.py:30
  192.6 36.8 %copy-start.18 = (bf16[768,1024]{1,0:T(8,128)(2,1)}, bf16[768,1024]{1,0:T(8,128)(2,1)S(1)}, u32[]{:S(2)}) copy-start(bf16[768,1024]{1,0:T(8,128)(2,1)S(1)} %collective-permute-done.5) | copy-start | bytes 4718596
  192.6 36.8 %collective-permute-start.6 = (bf16[768,1024]{1,0:T(8,128)(2,1)S(1)}, bf16[768,1024]{1,0:T(8,128)(2,1)}, u32[]{:S(2)}, u32[]{:S(2)}) collective-permute-start(bf16[768,1024]{1,0:T(8,128)(2,1)S(1)} %collective-permute-done.5), channel_id=1, source_target_pairs={{0,1},{1,2},{2,3},{3,4},{4,5},{5,6},{6,7},{7,8},{8,9},{9,10},{10,1... | collective-permute-start | bytes 4718600 | tf_op jit(solution)/shard_map/ppermute | solution.py:27
  226.2 46.9 %collective-permute-start.13 = (bf16[768,1024]{1,0:T(8,128)(2,1)}, bf16[768,1024]{1,0:T(8,128)(2,1)}, u32[]{:S(2)}, u32[]{:S(2)}) collective-permute-start(bf16[768,1024]{1,0:T(8,128)(2,1)} %collective-permute-done.12), channel_id=1, source_target_pairs={{1,0},{2,1},{3,2},{4,3},{5,4},{6,5},{7,6},{8,7},{9,8},{10,9},{11,1... | collective-permute-start | bytes 4718600 | tf_op jit(solution)/shard_map/ppermute | solution.py:30
  229.4 44.0 %collective-permute-start.7 = (bf16[768,1024]{1,0:T(8,128)(2,1)}, bf16[768,1024]{1,0:T(8,128)(2,1)}, u32[]{:S(2)}, u32[]{:S(2)}) collective-permute-start(bf16[768,1024]{1,0:T(8,128)(2,1)} %collective-permute-done.6), channel_id=1, source_target_pairs={{0,1},{1,2},{2,3},{3,4},{4,5},{5,6},{6,7},{7,8},{8,9},{9,10},{10,1... | collective-permute-start | bytes 4718600 | tf_op jit(solution)/shard_map/ppermute | solution.py:27
  273.1 27.1 %collective-permute-start.14 = (bf16[768,1024]{1,0:T(8,128)(2,1)}, bf16[768,1024]{1,0:T(8,128)(2,1)S(1)}, u32[]{:S(2)}, u32[]{:S(2)}) collective-permute-start(bf16[768,1024]{1,0:T(8,128)(2,1)} %collective-permute-done.13), channel_id=1, source_target_pairs={{1,0},{2,1},{3,2},{4,3},{5,4},{6,5},{7,6},{8,7},{9,8},{10,9},{11,1... | collective-permute-start | bytes 4718600 | tf_op jit(solution)/shard_map/ppermute | solution.py:30
  464.7 115.6 %reduce-scatter.5.cloned.1.call-start = ((), (), s32[]{:S(2)}) async-start(), calls=%async_computation.4 | async-start | bytes 786432 | tf_op jit(solution)/shard_map/reduce_scatter | solution.py:103
  (14 other events, 54.9 us)
Sparse Core Ops, SparseCore 0:
  66.9 77.5 all-gather.1
  464.8 99.4 reduce-scatter.2
  566.5 13.6 reduce-scatter.4
